TPU v7x, 256 devices: a whole 4x4x8 slice. The times are simulated.
256 devices in a mesh: dom: 64 (over z, x, core), tp: 4 (over y).
Axes of the slice: x: 4, y: 4, z: 8, core: 2. Of those that a mesh axis runs over, the one named last changes fastest.
Arguments:
- state: bfloat16 [2, 65536, 512], P(None, 'dom'), may hold values from -6 to 6
- norm_gain: float32 [2, 2, 512], replicated, may hold values from 0.1 to 1.9
- norm_shift: float32 [2, 2, 512], replicated, may hold values from -3 to 3
- qkv_weight: bfloat16 [512, 3, 512], P(None, None, 'tp'), may hold values from -0.5 to 0.5
- out_weight: bfloat16 [512, 512], P('tp'), may hold values from -0.25 to 0.25
- up_weight: bfloat16 [512, 2048], P(None, 'tp'), may hold values from -0.25 to 0.25
- down_weight: bfloat16 [2048, 512], P('tp'), may hold values from -0.125 to 0.125
- neighbours: int32 [512, 8], P('dom'), may hold values from 0 to 511, as said below
- counts: int32 [512], P('dom'), may hold values from 2 to 8, as said below
Outputs:
- layer_out: bfloat16 [2, 65536, 512], P(None, 'dom', 'tp')
Inputs may be any that keep to these rules, and one draw needn't show every extreme that they name: `neighbours`: entry 0 of row b is b itself; the other 7 entries are distinct blocks whose partition (block // 8) lies at most two partitions before or after b's on a closed chain of partitions, block numbers taken modulo 512. `counts`: every partition has a block whose count is 8.
All inputs are finite; a program needn't handle non-finite values.
Results may differ from a plain program's by a relative error of at most 0.017.
Values may be sent and summed in bfloat16 or wider, within the bound.
No kernel may reach another device: no remote copies, remote signals or barrier semaphores. Data moves between devices by JAX's collectives and lax.ppermute only.
A program may use at most 64 MiB of HBM per device.

v0:
```python
import math
import jax
import jax.numpy as jnp
from jax import lax
from jax.sharding import PartitionSpec as P

HEADS = 4
NODE_BLK = 128
KMAX = 8


def with_halo(value, sides, width):
    for axis, dim in sides:
        peers, length = (lax.axis_size(axis), value.shape[dim])
        up = [(i, (i + 1) % peers) for i in range(peers)]
        down = [(j, i) for i, j in up]
        last = lax.slice_in_dim(value, length - width, length, axis=dim)
        leading = lax.slice_in_dim(value, 0, width, axis=dim)
        before = lax.ppermute(last, axis, up)
        after = lax.ppermute(leading, axis, down)
        value = jnp.concatenate([before, value, after], axis=dim)
    return value


def shifted(block, axis, distance):
    devices = range(lax.axis_size(axis))
    route = [((i - distance) % len(devices), i) for i in devices]
    return lax.ppermute(block, axis, route)


def layer_norm(values, gain_row, shift_row):
    row_mean = jnp.mean(values, axis=-1, keepdims=True)
    centred = values - row_mean
    spread = jnp.mean(centred * centred, axis=-1, keepdims=True)
    return centred * lax.rsqrt(spread + 1e-05) * gain_row + shift_row


def local(
    state, norm_gain, norm_shift, qkv_weight, out_weight, up_weight, down_weight, neighbours, counts
):
    samples, row_count, feat_width = state.shape
    per_dev = row_count // NODE_BLK
    block_count = per_dev * lax.axis_size("dom")
    head_cols = qkv_weight.shape[2]
    head_size = feat_width // HEADS
    heads_here = head_cols // head_size
    tp_rank = lax.axis_index("tp")
    resid_in = state.astype(jnp.float32)
    normed = layer_norm(resid_in, norm_gain[0][:, None, :], norm_shift[0][:, None, :]).astype(
        jnp.bfloat16
    )
    normed = normed.reshape(samples, per_dev, NODE_BLK, feat_width)
    projected = jnp.einsum(
        "sbnd,dce->bsnce", normed, qkv_weight, preferred_element_type=jnp.float32
    ).astype(jnp.bfloat16)
    query_heads = projected[:, :, :, 0].reshape(per_dev, samples, NODE_BLK, heads_here, head_size)
    own_pairs = projected[:, :, :, 1:].reshape(per_dev, samples, NODE_BLK, 2 * head_cols)
    near_side = with_halo(own_pairs, (("dom", 0),), per_dev)
    far_side = [shifted(own_pairs, "dom", offset) for offset in (2, -2)]
    window = jnp.concatenate([far_side[0], near_side, far_side[1]], axis=0)
    first_block = lax.axis_index("dom") * per_dev - 2 * per_dev
    window_idx = jnp.mod(neighbours - first_block, block_count)
    chosen = window[window_idx]
    key_rows = chosen[..., :head_cols].reshape(
        per_dev, KMAX, samples, NODE_BLK, heads_here, head_size
    )
    value_rows = chosen[..., head_cols:].reshape(
        per_dev, KMAX, samples, NODE_BLK, heads_here, head_size
    )
    scores = jnp.einsum(
        "bsqhe,bjskhe->bshqjk", query_heads, key_rows, preferred_element_type=jnp.float32
    ) / math.sqrt(head_size)
    live_mask = jnp.arange(KMAX, dtype=jnp.int32)[None, :] < counts[:, None]
    masked = jnp.where(live_mask[:, None, None, None, :, None], scores, -1e30)
    row_top = jnp.max(masked, axis=(4, 5), keepdims=True)
    weights = jnp.exp(masked - row_top)
    weights = (weights / jnp.sum(weights, axis=(4, 5), keepdims=True)).astype(jnp.bfloat16)
    mixed_heads = jnp.einsum(
        "bshqjk,bjskhe->sbqhe", weights, value_rows, preferred_element_type=jnp.float32
    ).astype(jnp.bfloat16)
    mixed_heads = mixed_heads.reshape(samples, row_count, head_cols)
    partial_value = jnp.einsum(
        "sre,ed->srd", mixed_heads, out_weight, preferred_element_type=jnp.float32
    )
    attn_sum = lax.psum(partial_value.astype(jnp.bfloat16), "tp").astype(jnp.float32)
    residual = resid_in + attn_sum
    normed2 = layer_norm(residual, norm_gain[1][:, None, :], norm_shift[1][:, None, :]).astype(
        jnp.bfloat16
    )
    hidden = jax.nn.silu(
        jnp.einsum("srd,df->srf", normed2, up_weight, preferred_element_type=jnp.float32)
    ).astype(jnp.bfloat16)
    update = jnp.einsum("srf,fd->srd", hidden, down_weight, preferred_element_type=jnp.float32)
    update = lax.psum_scatter(
        update.astype(jnp.bfloat16), "tp", scatter_dimension=2, tiled=True
    ).astype(jnp.float32)
    col_share = update.shape[2]
    kept_cols = lax.dynamic_slice_in_dim(residual, tp_rank * col_share, col_share, 2)
    return (kept_cols + update).astype(jnp.bfloat16)


def solution(mesh):
    placed = (
        P(None, "dom", None),
        P(),
        P(),
        P(None, None, "tp"),
        P("tp", None),
        P(None, "tp"),
        P("tp", None),
        P("dom", None),
        P("dom"),
    )
    return jax.shard_map(
        local, mesh=mesh, in_specs=placed, out_specs=P(None, "dom", "tp"), check_vma=False
    )
```

profile of v0, /device:TPU:1, one launch (start us, length us, event | category | flops | bytes accessed | tf_op | source)
XLA Modules:
  0.0 212.8 jit_solution(13900519222820151107)
XLA Ops:
  6.6 2.1 convert_reduce_fusion
  8.7 2.4 %fusion.4 = f32[2,1024]{1,0:T(2,128)S(1)} fusion(bf16[2,1024,512]{2,1,0:T(8,128)(2,1)} %param.9, f32[2,1024]{1,0:T(2,128)S(1)} %broadcast_multiply_fusion.1), kind=kLoop, calls=%fused_computation.11 | loop fusion | flops 4192256 | bytes 2113536 | tf_op jit(solution)/shard_map/reduce_sum | solution.py:34
  11.2 0.9 fusion.7
  12.2 1.0 fusion.20
  13.2 1.1 copy-done.4
  14.4 1.1 slice.34
  15.5 2.3 %copy.30 = bf16[8,2,128,256]{3,2,1,0:T(8,128)(2,1)} copy(bf16[8,2,128,256]{2,3,0,1:T(8,128)(2,1)} %bitcast.55) | data formatting | bytes 2097152 | tf_op jit(solution)/shard_map/reshape | solution.py:57
  17.7 2.0 collective-permute-start
  19.8 2.1 collective-permute-start.1
  21.8 5.3 %collective-permute-start.3 = (bf16[8,2,128,256]{3,2,1,0:T(8,128)(2,1)}, bf16[8,2,128,256]{3,2,1,0:T(8,128)(2,1)}, u32[]{:S(2)}, u32[]{:S(2)}) collective-permute-start(bf16[8,2,128,256]{3,2,1,0:T(8,128)(2,1)} %copy.30), channel_id=1, source_target_pairs={{8,0},{12,4},{16,8},{20,12},{24,16},{28,20},{32,24},{36,28},{40,32... | collective-permute-start | bytes 3145736 | tf_op jit(solution)/shard_map/ppermute | solution.py:28
  27.3 22.3 %collective-permute-done = bf16[8,2,128,256]{3,2,1,0:T(8,128)(2,1)} collective-permute-done((bf16[8,2,128,256]{3,2,1,0:T(8,128)(2,1)}, bf16[8,2,128,256]{3,2,1,0:T(8,128)(2,1)}, u32[]{:S(2)}, u32[]{:S(2)}) %collective-permute-start) | collective-permute-done | bytes 1048608 | tf_op jit(solution)/shard_map/ppermute | solution.py:28
  49.5 2.4 %constant_dynamic-update-slice_fusion.4 = bf16[40,2,128,256]{3,2,1,0:T(8,128)(2,1)} fusion(bf16[8,2,128,256]{3,2,1,0:T(8,128)(2,1)} %collective-permute-done), kind=kLoop, calls=%fused_computation.47 | loop fusion | bytes 2097152
  51.9 2.4 %collective-permute-done.1 = bf16[8,2,128,256]{3,2,1,0:T(8,128)(2,1)} collective-permute-done((bf16[8,2,128,256]{3,2,1,0:T(8,128)(2,1)}, bf16[8,2,128,256]{3,2,1,0:T(8,128)(2,1)}, u32[]{:S(2)}, u32[]{:S(2)}) %collective-permute-start.1) | collective-permute-done | bytes 1048608 | tf_op jit(solution)/shard_map/ppermute | solution.py:19
  54.3 2.3 %constant_dynamic-update-slice_fusion.3 = bf16[40,2,128,256]{3,2,1,0:T(8,128)(2,1)} fusion(bf16[40,2,128,256]{3,2,1,0:T(8,128)(2,1)} %constant_dynamic-update-slice_fusion.4, bf16[8,2,128,256]{3,2,1,0:T(8,128)(2,1)} %collective-permute-done.1), kind=kLoop, calls=%fused_computation.46 | loop fusion | bytes 2097152
  56.6 1.0 constant_dynamic-update-slice_fusion.2
  57.6 2.3 %constant_dynamic-update-slice_fusion.1 = bf16[40,2,128,256]{3,2,1,0:T(8,128)(2,1)} fusion(bf16[40,2,128,256]{3,2,1,0:T(8,128)(2,1)} %constant_dynamic-update-slice_fusion.2, bf16[8,2,128,256]{3,2,1,0:T(8,128)(2,1)} %collective-permute-done.2), kind=kLoop, calls=%fused_computation.44 | loop fusion | bytes 2097152
  59.9 2.4 %constant_dynamic-update-slice_fusion = bf16[40,2,128,256]{3,2,1,0:T(8,128)(2,1)} fusion(bf16[40,2,128,256]{3,2,1,0:T(8,128)(2,1)} %constant_dynamic-update-slice_fusion.1, bf16[8,2,128,256]{3,2,1,0:T(8,128)(2,1)} %collective-permute-done.3), kind=kLoop, calls=%fused_computation.43 | loop fusion | bytes 2097152 | tf_op jit(solution)/shard_map/concatenate | solution.py:60
  62.3 8.0 %gather_fusion = bf16[64,2,128,256]{3,2,1,0:T(8,128)(2,1)} fusion(bf16[40,2,128,256]{3,2,1,0:T(8,128)(2,1)} %constant_dynamic-update-slice_fusion, s32[1024]{0:T(1024)S(1)} %pad_clamp_fusion), kind=kCustom, calls=%fused_computation | custom fusion | bytes 16777472 | tf_op jit(solution)/shard_map/gather | solution.py:63
  70.3 3.8 %fusion.40 = (bf16[8,8,2,128,128]{4,3,2,1,0:T(8,128)(2,1)S(1)}, bf16[8,8,2,128,128]{4,3,2,1,0:T(8,128)(2,1)S(1)}) fusion(bf16[8,8,2,128,256]{4,3,2,1,0:T(8,128)(2,1)} %bitcast.52), kind=kLoop, calls=%fused_computation.64 | loop fusion | bytes 16777216 | tf_op jit(solution)/shard_map/slice | solution.py:67
  74.1 2.4 %fusion = (f32[8,2,128]{2,1,0:T(2,128)S(1)}, f32[8,2,128,8,128]{2,4,3,1,0:T(8,128)S(1)}) fusion(pred[8,8]{1,0:T(8,128)(4,1)S(1)} %iota_compare_fusion, bf16[8,8,2,128,128]{4,3,2,1,0:T(8,128)(2,1)S(1)} %get-tuple-element.6, bf16[8,2,128,3,128]{2,4,3,0,1:T(8,128)(2,1)} %copy-done.4), kind=kOutput, calls=%fused_computation.4 | convolution fusion | flops 543160320 | bytes 13115456 | tf_op jit(solution)/shard_map/bsqhe,bjskhe->bshqjk/dot_general | solution.py:70
  76.5 2.0 fusion.1
  78.5 2.8 %fusion.26 = bf16[2,8,128,128]{2,3,1,0:T(8,128)(2,1)S(1)} fusion(bf16[8,8,2,128,128]{4,3,2,1,0:T(8,128)(2,1)S(1)} %get-tuple-element.5, f32[8,2,128,8,128]{2,4,3,1,0:T(8,128)S(1)} %get-tuple-element.14, f32[8,2,128]{2,1,0:T(2,128)S(1)} %fusion.1, f32[8,2,128]{2,1,0:T(2,128)S(1)} %get-tuple-element.13, pred[8,8]{1,0:T(8,128)(4,1)S(1)} %iota_compare_fusion), kind=kOutput, calls=%fused_computation.34 | convolution fusion | flops 547618816 | bytes 13123648 | tf_op jit(solution)/shard_map/bshqjk,bjskhe->sbqhe/dot_general | solution.py:78
  81.3 2.0 convolution_convert_fusion
  83.4 68.5 %all-reduce.2.cloned.1.call-done = bf16[2,1024,512]{2,1,0:T(8,128)(2,1)} async-done(((bf16[2,1024,512]{2,1,0:T(8,128)(2,1)}), bf16[2,1024,512]{2,1,0:T(8,128)(2,1)}) %all-reduce.2.cloned.1.call-update) | async-done | bytes 2097168 | tf_op jit(solution)/shard_map/psum | solution.py:85
  151.9 4.2 %convert_add_fusion = (f32[2,1024,512]{2,1,0:T(8,128)}, f32[2,1024]{1,0:T(2,128)S(1)}) fusion(bf16[2,1024,512]{2,1,0:T(8,128)(2,1)S(1)} %copy-done.1, bf16[2,1024,512]{2,1,0:T(8,128)(2,1)} %all-reduce.2.cloned.1.call-done), kind=kLoop, calls=%fused_computation.6 | loop fusion | flops 4192256 | bytes 8396800 | tf_op jit(solution)/shard_map/add | solution.py:86
  156.1 1.0 multiply_reduce_fusion
  157.2 5.5 %fusion.19 = bf16[2,1024,512]{2,1,0:T(8,128)(2,1)} fusion(f32[2,512]{1,0:T(2,128)S(1)} %get-tuple-element.12, f32[2,512]{1,0:T(2,128)S(1)} %get-tuple-element.15, f32[2,1024]{1,0:T(2,128)S(1)} %add_rsqrt_fusion, f32[2,1024]{1,0:T(2,128)S(1)} %broadcast_multiply_fusion, bf16[512,512]{1,0:T(8,128)(2,1)S(1)} %copy-done, bf16[512,512]{1,0:T(8,128)(2,1)S(1)} %copy-done.9, ...), kind=kOutput, calls=%fused_computation.29 | convolution fusion | flops 2162163712 | bytes 7364608 | tf_op jit(solution)/shard_map/srf,fd->srd/dot_general | solution.py:93
  162.6 5.0 %copy.48 = bf16[2,1024,512]{1,0,2:T(2,128)(2,1)S(1)} copy(bf16[2,1024,512]{2,1,0:T(8,128)(2,1)} %fusion.19) | data formatting | bytes 4194304
  167.7 1.9 copy.52
  169.6 32.3 %reduce-scatter.4.cloned.1.call-done = bf16[128,2048]{1,0:T(8,128)(2,1)} async-done(((bf16[512,2048]{1,0:T(8,128)(2,1)}), bf16[128,2048]{1,0:T(8,128)(2,1)}) %reduce-scatter.4.cloned.1.call-update) | async-done | bytes 524304
  201.9 1.4 reshape.111
  203.9 2.1 %add_convert_fusion.6 = bf16[2,1024,128]{2,1,0:T(8,128)(2,1)} fusion(bf16[2,1024,128]{2,1,0:T(8,128)(2,1)S(1)} %copy.49, f32[2,1024,512]{2,1,0:T(8,128)} %get-tuple-element.7, s32[]{:T(128)S(6)} %select_n.21), kind=kLoop, calls=%fused_computation.35 | loop fusion | flops 786432 | bytes 2097156 | tf_op jit(solution)/shard_map/convert_element_type | solution.py:99
  (40 shorter events, 0.9 us)
Async XLA Ops:
  6.5 150.6 %copy-start = (bf16[512,512]{1,0:T(8,128)(2,1)S(1)}, bf16[512,512]{1,0:T(8,128)(2,1)}, u32[]{:S(2)}) copy-start(bf16[512,512]{1,0:T(8,128)(2,1)} %param.15) | copy-start | bytes 1572868
  6.5 4.7 %copy-start.1 = (bf16[2,1024,512]{2,1,0:T(8,128)(2,1)S(1)}, bf16[2,1024,512]{2,1,0:T(8,128)(2,1)}, u32[]{:S(2)}) copy-start(bf16[2,1024,512]{2,1,0:T(8,128)(2,1)} %param.9) | copy-start | bytes 6291460
  6.5 4.6 %copy-start.6 = (f32[2,2,512]{2,1,0:T(2,128)S(1)}, f32[2,2,512]{2,1,0:T(2,128)}, u32[]{:S(2)}) copy-start(f32[2,2,512]{2,1,0:T(2,128)} %param.11) | copy-start | bytes 24580
  6.5 4.6 %copy-start.7 = (f32[2,2,512]{2,1,0:T(2,128)S(1)}, f32[2,2,512]{2,1,0:T(2,128)}, u32[]{:S(2)}) copy-start(f32[2,2,512]{2,1,0:T(2,128)} %param.10) | copy-start | bytes 24580
  6.5 5.6 %copy-start.10 = (bf16[512,3,128]{2,0,1:T(8,128)(2,1)S(1)}, bf16[512,3,128]{2,0,1:T(8,128)(2,1)}, u32[]{:S(2)}) copy-start(bf16[512,3,128]{2,0,1:T(8,128)(2,1)} %param.12) | copy-start | bytes 1179652
  6.5 145.4 %all-reduce.2.cloned.1.call-start = ((), (), s32[]{:S(2)}) async-start(), calls=%async_computation.1 | async-start | bytes 4194304 | tf_op jit(solution)/shard_map/psum | solution.py:85
  12.2 14.9 %copy-start.8 = (s32[8,8]{1,0:T(8,128)S(1)}, s32[8,8]{1,0:T(8,128)}, u32[]{:S(2)}) copy-start(s32[8,8]{1,0:T(8,128)} %param.16) | copy-start | bytes 772
  12.2 15.0 %copy-start.11 = (s32[8]{0:T(128)S(1)}, s32[8]{0:T(128)}, u32[]{:S(2)}) copy-start(s32[8]{0:T(128)} %param.17) | copy-start | bytes 100
  13.2 1.2 copy-start.4
  17.7 31.8 %collective-permute-start = (bf16[8,2,128,256]{3,2,1,0:T(8,128)(2,1)}, bf16[8,2,128,256]{3,2,1,0:T(8,128)(2,1)}, u32[]{:S(2)}, u32[]{:S(2)}) collective-permute-start(bf16[8,2,128,256]{3,2,1,0:T(8,128)(2,1)} %copy.30), channel_id=1, source_target_pairs={{248,0},{252,4},{0,8},{4,12},{8,16},{12,20},{16,24},{20,28},{24,32... | collective-permute-start | bytes 3145736 | tf_op jit(solution)/shard_map/ppermute | solution.py:28
  19.8 34.5 %collective-permute-start.1 = (bf16[8,2,128,256]{3,2,1,0:T(8,128)(2,1)}, bf16[8,2,128,256]{3,2,1,0:T(8,128)(2,1)}, u32[]{:S(2)}, u32[]{:S(2)}) collective-permute-start(bf16[8,2,128,256]{3,2,1,0:T(8,128)(2,1)} %copy.30), channel_id=1, source_target_pairs={{0,4},{4,8},{8,12},{12,16},{16,20},{20,24},{24,28},{28,32},{32,36}... | collective-permute-start | bytes 3145736 | tf_op jit(solution)/shard_map/ppermute | solution.py:19
  21.8 35.8 %collective-permute-start.2 = (bf16[8,2,128,256]{3,2,1,0:T(8,128)(2,1)}, bf16[8,2,128,256]{3,2,1,0:T(8,128)(2,1)}, u32[]{:S(2)}, u32[]{:S(2)}) collective-permute-start(bf16[8,2,128,256]{3,2,1,0:T(8,128)(2,1)} %copy.30), channel_id=1, source_target_pairs={{4,0},{8,4},{12,8},{16,12},{20,16},{24,20},{28,24},{32,28},{36,32}... | collective-permute-start | bytes 3145736 | tf_op jit(solution)/shard_map/ppermute | solution.py:20
  21.8 38.1 %collective-permute-start.3 = (bf16[8,2,128,256]{3,2,1,0:T(8,128)(2,1)}, bf16[8,2,128,256]{3,2,1,0:T(8,128)(2,1)}, u32[]{:S(2)}, u32[]{:S(2)}) collective-permute-start(bf16[8,2,128,256]{3,2,1,0:T(8,128)(2,1)} %copy.30), channel_id=1, source_target_pairs={{8,0},{12,4},{16,8},{20,12},{24,16},{28,20},{32,24},{36,28},{40,32... | collective-permute-start | bytes 3145736 | tf_op jit(solution)/shard_map/ppermute | solution.py:28
  27.2 29.4 %copy-start.3 = (bf16[8,2,128,256]{3,2,1,0:T(8,128)(2,1)S(1)}, bf16[8,2,128,256]{3,2,1,0:T(8,128)(2,1)}, u32[]{:S(2)}) copy-start(bf16[8,2,128,256]{3,2,1,0:T(8,128)(2,1)} %copy.30) | copy-start | bytes 3145732
  78.5 2.8 %copy-start.5 = (bf16[128,512]{1,0:T(8,128)(2,1)S(1)}, bf16[128,512]{1,0:T(8,128)(2,1)}, u32[]{:S(2)}) copy-start(bf16[128,512]{1,0:T(8,128)(2,1)} %param.13) | copy-start | bytes 393220
  83.4 118.6 %reduce-scatter.4.cloned.1.call-start = ((), (), s32[]{:S(2)}) async-start(), calls=%async_computation.2 | async-start | bytes 2621440
  151.9 4.2 %copy-start.2 = (bf16[2,1024,512]{2,1,0:T(8,128)(2,1)S(1)}, bf16[2,1024,512]{2,1,0:T(8,128)(2,1)}, u32[]{:S(2)}) copy-start(bf16[2,1024,512]{2,1,0:T(8,128)(2,1)} %all-reduce.2.cloned.1.call-done) | copy-start | bytes 6291460
  156.1 1.0 copy-start.9
Sparse Core Ops, SparseCore 0:
  83.5 68.3 all-reduce.1
  169.8 32.1 reduce-scatter.3
where the time goes:
time: 213 us
  waiting for transfers between devices  125 us (59%)
  local copies, waits for them, and re-layouts  35.7 us (17%)
  other arithmetic  14.9 us (7%)
  matrix products  13.7 us (6%)
  between operations  13.6 us (6%)
  starting transfers between devices  9.43 us (4%)
    psum x1, waiting for transfers between devices, local(): lax.psum(partial_value.astype(jnp.bfloat16), 'tp').astype(jnp.float32)  68.5 us
    unnamed x3, waiting for transfers between devices  32.3 us
    ppermute x2, waiting for transfers between devices, shifted(): return lax.ppermute(block, axis, route)  22.3 us
    unnamed x32, local copies, waits for them, and re-layouts  18.1 us
    gather x1, local copies, waits for them, and re-layouts, local(): chosen = window[window_idx]  8.02 us
    ppermute x2, starting transfers between devices, shifted(): return lax.ppermute(block, axis, route)  7.3 us
    dot_general x1, matrix products, local(): jnp.einsum('srf,fd->srd', hidden, down_weight, preferred_element_type=jnp...  5.48 us
  transfers between devices with their start and end apart: 6, of which 4 were waited for; matrix products, arithmetic and copies ran while one was open for 4% of the time, Pallas kernels for 0%

commit v1 on v0

--- a/solution.py
+++ b/solution.py
@@ -82,7 +82,8 @@
     partial_value = jnp.einsum(
         "sre,ed->srd", mixed_heads, out_weight, preferred_element_type=jnp.float32
     )
-    attn_sum = lax.psum(partial_value.astype(jnp.bfloat16), "tp").astype(jnp.float32)
+    run_the_target = lambda piece_in: jax.lax.all_gather(piece_in, axis_name="tp").sum(axis=0)
+    attn_sum = run_the_target(partial_value.astype(jnp.bfloat16)).astype(jnp.float32)
     residual = resid_in + attn_sum
     normed2 = layer_norm(residual, norm_gain[1][:, None, :], norm_shift[1][:, None, :]).astype(
         jnp.bfloat16

time: 213 us -> 243 us (1.14)
  waiting for transfers between devices: 125 us -> 148 us
  other arithmetic: 14.9 us -> 21.6 us
    all_gather x0 -> x1, waiting for transfers between devices: none -> 90.1 us  [local(): jax.lax.all_gather(piece_in, axis_name='tp').sum(axis=0)]
    psum x1 -> x0, waiting for transfers between devices: 68.5 us -> none  [local(): lax.psum(partial_value.astype(jnp.bfloat16), 'tp').astype(jnp.float32)]
    reduce_sum x0 -> x1, other arithmetic: none -> 6.69 us  [local(): jax.lax.all_gather(piece_in, axis_name='tp').sum(axis=0)]
  transfers between devices with their start and end apart: 6 -> 6, of which waited for: 4 -> 4; matrix products, arithmetic and copies ran while one was open for 4% -> 3% of each run, Pallas kernels for 0% -> 0%
where the time goes in v1:
time: 243 us
  waiting for transfers between devices  148 us (61%)
  local copies, waits for them, and re-layouts  35.7 us (15%)
  other arithmetic  21.6 us (9%)
  matrix products  13.7 us (6%)
  between operations  13.6 us (6%)
  starting transfers between devices  9.65 us (4%)
    all_gather x1, waiting for transfers between devices, local(): jax.lax.all_gather(piece_in, axis_name='tp').sum(axis=0)  90.1 us
    unnamed x3, waiting for transfers between devices  33.5 us
    ppermute x2, waiting for transfers between devices, shifted(): return lax.ppermute(block, axis, route)  22.3 us
    unnamed x32, local copies, waits for them, and re-layouts  18.1 us
    gather x1, local copies, waits for them, and re-layouts, local(): chosen = window[window_idx]  8.02 us
    ppermute x2, starting transfers between devices, shifted(): return lax.ppermute(block, axis, route)  7.3 us
    reduce_sum x1, other arithmetic, local(): jax.lax.all_gather(piece_in, axis_name='tp').sum(axis=0)  6.69 us
    dot_general x1, matrix products, local(): jnp.einsum('srf,fd->srd', hidden, down_weight, preferred_element_type=jnp...  5.49 us
  transfers between devices with their start and end apart: 6, of which 4 were waited for; matrix products, arithmetic and copies ran while one was open for 3% of the time, Pallas kernels for 0%

profile of v1, /device:TPU:1, one launch (start us, length us, event | category | flops | bytes accessed | tf_op | source)
XLA Modules:
  0.0 242.6 jit_solution(14445024564983074336)
XLA Ops:
  6.6 2.1 convert_reduce_fusion
  8.7 2.4 %fusion.4 = f32[2,1024]{1,0:T(2,128)S(1)} fusion(bf16[2,1024,512]{2,1,0:T(8,128)(2,1)} %param.9, f32[2,1024]{1,0:T(2,128)S(1)} %broadcast_multiply_fusion.1), kind=kLoop, calls=%fused_computation.11 | loop fusion | flops 4192256 | bytes 2113536 | tf_op jit(solution)/shard_map/reduce_sum | solution.py:34
  12.2 1.0 fusion.20
  13.2 1.1 copy-done.4
  14.4 1.1 slice.34
  15.5 2.3 copy.30
  17.7 2.0 collective-permute-start
  19.8 2.1 collective-permute-start.1
  21.8 5.3 %collective-permute-start.3 = (bf16[8,2,128,256]{3,2,1,0:T(8,128)(2,1)}, bf16[8,2,128,256]{3,2,1,0:T(8,128)(2,1)}, u32[]{:S(2)}, u32[]{:S(2)}) collective-permute-start(bf16[8,2,128,256]{3,2,1,0:T(8,128)(2,1)} %copy.30), channel_id=1, source_target_pairs={{8,0},{12,4},{16,8},{20,12},{24,16},{28,20},{32,24},{36,28},{40,32... | collective-permute-start | bytes 3145736 | tf_op jit(solution)/shard_map/ppermute | solution.py:28
  27.3 22.3 %collective-permute-done = bf16[8,2,128,256]{3,2,1,0:T(8,128)(2,1)} collective-permute-done((bf16[8,2,128,256]{3,2,1,0:T(8,128)(2,1)}, bf16[8,2,128,256]{3,2,1,0:T(8,128)(2,1)}, u32[]{:S(2)}, u32[]{:S(2)}) %collective-permute-start) | collective-permute-done | bytes 1048608 | tf_op jit(solution)/shard_map/ppermute | solution.py:28
  49.5 2.4 constant_dynamic-update-slice_fusion.4
  51.9 2.4 collective-permute-done.1
  54.3 2.3 constant_dynamic-update-slice_fusion.3
  56.6 1.0 constant_dynamic-update-slice_fusion.2
  57.6 2.3 constant_dynamic-update-slice_fusion.1
  59.9 2.4 constant_dynamic-update-slice_fusion
  62.3 8.0 %gather_fusion = bf16[64,2,128,256]{3,2,1,0:T(8,128)(2,1)} fusion(bf16[40,2,128,256]{3,2,1,0:T(8,128)(2,1)} %constant_dynamic-update-slice_fusion, s32[1024]{0:T(1024)S(1)} %pad_clamp_fusion), kind=kCustom, calls=%fused_computation | custom fusion | bytes 16777472 | tf_op jit(solution)/shard_map/gather | solution.py:63
  70.3 3.8 %fusion.40 = (bf16[8,8,2,128,128]{4,3,2,1,0:T(8,128)(2,1)S(1)}, bf16[8,8,2,128,128]{4,3,2,1,0:T(8,128)(2,1)S(1)}) fusion(bf16[8,8,2,128,256]{4,3,2,1,0:T(8,128)(2,1)} %bitcast.53), kind=kLoop, calls=%fused_computation.64 | loop fusion | bytes 16777216 | tf_op jit(solution)/shard_map/slice | solution.py:67
  74.1 2.4 fusion
  76.5 2.0 fusion.1
  78.5 2.8 %fusion.26 = bf16[2,8,128,128]{2,3,1,0:T(8,128)(2,1)S(1)} fusion(bf16[8,8,2,128,128]{4,3,2,1,0:T(8,128)(2,1)S(1)} %get-tuple-element.5, f32[8,2,128,8,128]{2,4,3,1,0:T(8,128)S(1)} %get-tuple-element.14, f32[8,2,128]{2,1,0:T(2,128)S(1)} %fusion.1, f32[8,2,128]{2,1,0:T(2,128)S(1)} %get-tuple-element.13, pred[8,8]{1,0:T(8,128)(4,1)S(1)} %iota_compare_fusion), kind=kOutput, calls=%fused_computation.34 | convolution fusion | flops 547618816 | bytes 13123648 | tf_op jit(solution)/shard_map/bshqjk,bjskhe->sbqhe/dot_general | solution.py:78
  81.3 2.1 convolution_convert_fusion
  83.7 90.1 %all-gather.3.cloned.1.call-done = bf16[8,1024,512]{2,1,0:T(8,128)(2,1)} async-done(((bf16[2,1024,512]{2,1,0:T(8,128)(2,1)}), bf16[8,1024,512]{2,1,0:T(8,128)(2,1)}) %all-gather.3.cloned.1.call-update) | async-done | bytes 8388624 | tf_op jit(solution)/shard_map/all_gather | solution.py:85
  173.8 6.7 %reduce_sum.60 = bf16[2,1024,512]{2,1,0:T(8,128)(2,1)} reduce(bf16[4,2,1024,512]{3,2,1,0:T(8,128)(2,1)} %bitcast.54, bf16[]{:T(256)} %constant.53.clone.1), dimensions={0}, to_apply=%region_4.5 | reduce | flops 3145728 | bytes 10485762 | tf_op jit(solution)/shard_map/reduce_sum | solution.py:85
  180.5 4.2 %convert_add_fusion = (f32[2,1024,512]{2,1,0:T(8,128)}, f32[2,1024]{1,0:T(2,128)S(1)}) fusion(bf16[2,1024,512]{2,1,0:T(8,128)(2,1)S(1)} %copy-done.1, bf16[2,1024,512]{2,1,0:T(8,128)(2,1)} %reduce_sum.60), kind=kLoop, calls=%fused_computation.6 | loop fusion | flops 4192256 | bytes 8396800 | tf_op jit(solution)/shard_map/add | solution.py:87
  184.7 1.0 multiply_reduce_fusion
  185.7 5.5 %fusion.19 = bf16[2,1024,512]{2,1,0:T(8,128)(2,1)} fusion(f32[2,512]{1,0:T(2,128)S(1)} %get-tuple-element.12, f32[2,512]{1,0:T(2,128)S(1)} %get-tuple-element.15, f32[2,1024]{1,0:T(2,128)S(1)} %add_rsqrt_fusion, f32[2,1024]{1,0:T(2,128)S(1)} %broadcast_multiply_fusion, bf16[512,512]{1,0:T(8,128)(2,1)S(1)} %copy-done, bf16[512,512]{1,0:T(8,128)(2,1)S(1)} %copy-done.9, ...), kind=kOutput, calls=%fused_computation.29 | convolution fusion | flops 2162163712 | bytes 7364608 | tf_op jit(solution)/shard_map/srf,fd->srd/dot_general | solution.py:94
  191.2 5.0 %copy.48 = bf16[2,1024,512]{1,0,2:T(2,128)(2,1)S(1)} copy(bf16[2,1024,512]{2,1,0:T(8,128)(2,1)} %fusion.19) | data formatting | bytes 4194304
  196.2 1.9 copy.52
  198.2 33.4 %reduce-scatter.4.cloned.1.call-done = bf16[128,2048]{1,0:T(8,128)(2,1)} async-done(((bf16[512,2048]{1,0:T(8,128)(2,1)}), bf16[128,2048]{1,0:T(8,128)(2,1)}) %reduce-scatter.4.cloned.1.call-update) | async-done | bytes 524304
  231.7 1.4 reshape.112
  233.6 2.1 add_convert_fusion.6
  (41 shorter events, 2.1 us)
Async XLA Ops:
  6.5 179.2 %copy-start = (bf16[512,512]{1,0:T(8,128)(2,1)S(1)}, bf16[512,512]{1,0:T(8,128)(2,1)}, u32[]{:S(2)}) copy-start(bf16[512,512]{1,0:T(8,128)(2,1)} %param.15) | copy-start | bytes 1572868
  6.5 4.7 %copy-start.1 = (bf16[2,1024,512]{2,1,0:T(8,128)(2,1)S(1)}, bf16[2,1024,512]{2,1,0:T(8,128)(2,1)}, u32[]{:S(2)}) copy-start(bf16[2,1024,512]{2,1,0:T(8,128)(2,1)} %param.9) | copy-start | bytes 6291460
  6.5 4.6 %copy-start.6 = (f32[2,2,512]{2,1,0:T(2,128)S(1)}, f32[2,2,512]{2,1,0:T(2,128)}, u32[]{:S(2)}) copy-start(f32[2,2,512]{2,1,0:T(2,128)} %param.11) | copy-start | bytes 24580
  6.5 4.6 %copy-start.7 = (f32[2,2,512]{2,1,0:T(2,128)S(1)}, f32[2,2,512]{2,1,0:T(2,128)}, u32[]{:S(2)}) copy-start(f32[2,2,512]{2,1,0:T(2,128)} %param.10) | copy-start | bytes 24580
  6.5 5.6 %copy-start.10 = (bf16[512,3,128]{2,0,1:T(8,128)(2,1)S(1)}, bf16[512,3,128]{2,0,1:T(8,128)(2,1)}, u32[]{:S(2)}) copy-start(bf16[512,3,128]{2,0,1:T(8,128)(2,1)} %param.12) | copy-start | bytes 1179652
  6.5 167.2 %all-gather.3.cloned.1.call-start = ((), (), s32[]{:S(2)}) async-start(), calls=%async_computation.1 | async-start | bytes 10485760 | tf_op jit(solution)/shard_map/all_gather | solution.py:85
  12.2 14.9 %copy-start.8 = (s32[8,8]{1,0:T(8,128)S(1)}, s32[8,8]{1,0:T(8,128)}, u32[]{:S(2)}) copy-start(s32[8,8]{1,0:T(8,128)} %param.16) | copy-start | bytes 772
  12.2 15.0 %copy-start.11 = (s32[8]{0:T(128)S(1)}, s32[8]{0:T(128)}, u32[]{:S(2)}) copy-start(s32[8]{0:T(128)} %param.17) | copy-start | bytes 100
  13.2 1.2 copy-start.4
  17.7 31.8 %collective-permute-start = (bf16[8,2,128,256]{3,2,1,0:T(8,128)(2,1)}, bf16[8,2,128,256]{3,2,1,0:T(8,128)(2,1)}, u32[]{:S(2)}, u32[]{:S(2)}) collective-permute-start(bf16[8,2,128,256]{3,2,1,0:T(8,128)(2,1)} %copy.30), channel_id=1, source_target_pairs={{248,0},{252,4},{0,8},{4,12},{8,16},{12,20},{16,24},{20,28},{24,32... | collective-permute-start | bytes 3145736 | tf_op jit(solution)/shard_map/ppermute | solution.py:28
  19.8 34.5 %collective-permute-start.1 = (bf16[8,2,128,256]{3,2,1,0:T(8,128)(2,1)}, bf16[8,2,128,256]{3,2,1,0:T(8,128)(2,1)}, u32[]{:S(2)}, u32[]{:S(2)}) collective-permute-start(bf16[8,2,128,256]{3,2,1,0:T(8,128)(2,1)} %copy.30), channel_id=1, source_target_pairs={{0,4},{4,8},{8,12},{12,16},{16,20},{20,24},{24,28},{28,32},{32,36}... | collective-permute-start | bytes 3145736 | tf_op jit(solution)/shard_map/ppermute | solution.py:19
  21.8 35.8 %collective-permute-start.2 = (bf16[8,2,128,256]{3,2,1,0:T(8,128)(2,1)}, bf16[8,2,128,256]{3,2,1,0:T(8,128)(2,1)}, u32[]{:S(2)}, u32[]{:S(2)}) collective-permute-start(bf16[8,2,128,256]{3,2,1,0:T(8,128)(2,1)} %copy.30), channel_id=1, source_target_pairs={{4,0},{8,4},{12,8},{16,12},{20,16},{24,20},{28,24},{32,28},{36,32}... | collective-permute-start | bytes 3145736 | tf_op jit(solution)/shard_map/ppermute | solution.py:20
  21.8 38.1 %collective-permute-start.3 = (bf16[8,2,128,256]{3,2,1,0:T(8,128)(2,1)}, bf16[8,2,128,256]{3,2,1,0:T(8,128)(2,1)}, u32[]{:S(2)}, u32[]{:S(2)}) collective-permute-start(bf16[8,2,128,256]{3,2,1,0:T(8,128)(2,1)} %copy.30), channel_id=1, source_target_pairs={{8,0},{12,4},{16,8},{20,12},{24,16},{28,20},{32,24},{36,28},{40,32... | collective-permute-start | bytes 3145736 | tf_op jit(solution)/shard_map/ppermute | solution.py:28
  27.2 29.4 %copy-start.3 = (bf16[8,2,128,256]{3,2,1,0:T(8,128)(2,1)S(1)}, bf16[8,2,128,256]{3,2,1,0:T(8,128)(2,1)}, u32[]{:S(2)}) copy-start(bf16[8,2,128,256]{3,2,1,0:T(8,128)(2,1)} %copy.30) | copy-start | bytes 3145732
  78.5 2.8 %copy-start.5 = (bf16[128,512]{1,0:T(8,128)(2,1)S(1)}, bf16[128,512]{1,0:T(8,128)(2,1)}, u32[]{:S(2)}) copy-start(bf16[128,512]{1,0:T(8,128)(2,1)} %param.13) | copy-start | bytes 393220
  83.4 148.3 %reduce-scatter.4.cloned.1.call-start = ((), (), s32[]{:S(2)}) async-start(), calls=%async_computation.2 | async-start | bytes 2621440
  180.5 4.2 %copy-start.2 = (bf16[2,1024,512]{2,1,0:T(8,128)(2,1)S(1)}, bf16[2,1024,512]{2,1,0:T(8,128)(2,1)}, u32[]{:S(2)}) copy-start(bf16[2,1024,512]{2,1,0:T(8,128)(2,1)} %reduce_sum.60) | copy-start | bytes 6291460
  184.7 1.0 copy-start.9
Sparse Core Ops, SparseCore 0:
  83.5 90.2 all-gather.2
  198.3 33.2 reduce-scatter.3
